TPU v7x, 256 devices: a whole 4x4x8 slice. The times are simulated.
256 devices in a mesh: pipe: 8 (over y, core), expert: 32 (over x, z).
Axes of the slice: x: 4, y: 4, z: 8, core: 2. Of those that a mesh axis runs over, the one named last changes fastest.
Arguments:
- state: bfloat16 [8, 1536, 2048], P('pipe', 'expert'), may hold values from -6 to 6
- route_ids: int32 [3, 8, 1536, 8], P(None, 'pipe', 'expert'), may hold values from 0 to 31, all different within a row; in each aligned block of 48 rows (0 to 47, 48 to 95, ..., all dimensions but the last counted through in order) at most 16 rows name the same one
- route_weights: float32 [3, 8, 1536, 8], P(None, 'pipe', 'expert'), may hold values from 0.02 to 0.3
- norm_gain: float32 [8, 2048], P('pipe'), may hold values from 0.1 to 1.9
- w_gate: bfloat16 [8, 32, 2048, 768], P('pipe', 'expert'), may hold values from -0.125 to 0.125
- w_up: bfloat16 [8, 32, 2048, 768], P('pipe', 'expert'), may hold values from -0.125 to 0.125
- w_down: bfloat16 [8, 32, 768, 2048], P('pipe', 'expert'), may hold values from -0.21875 to 0.21875
Outputs:
- final_state: bfloat16 [8, 1536, 2048], P('pipe', 'expert')
Inputs may be any that keep to these rules, and one draw needn't show every extreme that they name: `route_ids`: each token names 8 different experts. In the routes of one device (a block of 48 tokens of one step and section) no expert is named more than 16 times, and in every draw some block names an expert exactly 16 times.
All inputs are finite; a program needn't handle non-finite values.
Results may differ from a plain program's by a relative error of at most 0.0065.
Values may be sent and summed in bfloat16 or wider, within the bound.
No kernel may reach another device: no remote copies, remote signals or barrier semaphores. Data moves between devices by JAX's collectives and lax.ppermute only.
A program may use at most 64 MiB of HBM per device.

v0:
```python
import jax
import jax.numpy as jnp
from jax import lax
from jax.sharding import PartitionSpec as P


def shifted(array, axis, by):
    size = lax.axis_size(axis)
    return lax.ppermute(array, axis, [(i, (i + by) % size) for i in range(size)])


def expert_ffn(rows, gate_weight, up_weight, down_weight):
    shape = rows.shape
    flat = rows.reshape(-1, shape[-1])
    gate = jnp.dot(flat, gate_weight, preferred_element_type=jnp.float32)
    upper = jnp.dot(flat, up_weight, preferred_element_type=jnp.float32)
    hidden = (jax.nn.silu(gate) * upper).astype(jnp.bfloat16)
    output = jnp.dot(hidden, down_weight, preferred_element_type=jnp.float32).astype(jnp.bfloat16)
    return output.reshape(shape[:-1] + (down_weight.shape[1],))


def shards(state, route_ids, route_weights, norm_gain, w_gate, w_up, w_down):
    experts = lax.axis_size("expert")
    owner = lax.axis_index("expert")
    panel_rows = state.shape[1]
    width = state.shape[2]
    chosen = route_ids.shape[3]
    capacity = min(panel_rows, 4 * panel_rows * chosen // (3 * experts))
    gain = norm_gain[0]
    gate_weight = w_gate[0, 0]
    up_weight = w_up[0, 0]
    down_weight = w_down[0, 0]
    panel = state[0]
    for tick_index in range(route_ids.shape[0]):
        section_ids = route_ids[tick_index, 0]
        section_wts = route_weights[tick_index, 0]
        widened = panel.astype(jnp.float32)
        scale = lax.rsqrt(jnp.mean(widened * widened, axis=-1, keepdims=True) + 1e-06)
        normed = (widened * scale * gain).astype(jnp.bfloat16)
        matches = (section_ids.reshape(-1)[:, None] == jnp.arange(experts, dtype=jnp.int32)).astype(
            jnp.int32
        )
        ranks = jnp.cumsum(matches, axis=0) - 1
        slot_of = jnp.sum(ranks * matches, axis=1)
        position = section_ids.reshape(-1) * capacity + slot_of
        all_rows, all_ids = (
            lax.all_gather(normed, "expert", axis=0, tiled=True),
            lax.all_gather(section_ids, "expert", axis=0, tiled=True),
        )
        hit_token = jnp.sum((all_ids == owner).astype(jnp.int32), axis=1)
        hit_blocks = hit_token.reshape(experts, panel_rows)
        block_rank = jnp.cumsum(hit_blocks, axis=1) - 1
        sources = jnp.arange(experts, dtype=jnp.int32)[:, None]
        target = jnp.where(
            hit_blocks > 0, sources * capacity + block_rank, experts * capacity
        ).reshape(-1)
        every_token = jnp.arange(experts * panel_rows, dtype=jnp.int32)
        slot_token = (
            jnp.zeros((experts * capacity,), jnp.int32).at[target].set(every_token, mode="drop")
        )
        filled = jnp.zeros((experts * capacity,), jnp.int32).at[target].set(1, mode="drop")
        incoming = jnp.where(filled[:, None] > 0, all_rows[slot_token], jnp.zeros((), jnp.bfloat16))
        results = expert_ffn(
            incoming.reshape(experts, capacity, width), gate_weight, up_weight, down_weight
        )
        returned = lax.all_to_all(results, "expert", split_axis=0, concat_axis=0, tiled=True)
        picked = returned.reshape(experts * capacity, width)[position].reshape(
            panel_rows, chosen, width
        )
        combined = jnp.sum(section_wts[:, :, None] * picked.astype(jnp.float32), axis=1)
        updated = (widened + combined).astype(jnp.bfloat16)
        panel = shifted(updated, "pipe", 1)
    return panel[None]


def solution(mesh):
    placed = (
        P("pipe", "expert", None),
        P(None, "pipe", "expert", None),
        P(None, "pipe", "expert", None),
        P("pipe", None),
        P("pipe", "expert", None, None),
        P("pipe", "expert", None, None),
        P("pipe", "expert", None, None),
    )
    return jax.shard_map(
        shards, mesh=mesh, in_specs=placed, out_specs=P("pipe", "expert", None), check_vma=False
    )
```

profile of v0, /device:TPU:32, one launch (start us, length us, event | category | flops | bytes accessed | tf_op | source)
XLA Modules:
  0.0 698.8 jit_solution(3878133319197394416)
XLA Ops:
  10.5 52.2 %all-gather.1 = s32[1,1,1536,8]{3,1,0,2:T(1,128)S(1)} all-gather(s32[1,1,48,8]{3,1,0,2:T(1,128)S(1)} %copy.36), channel_id=3, replica_groups=mesh['pipe'=8,'expert'=32] {'expert'}, dimensions={2}, use_global_device_ids=true | all-gather | bytes 50688 | tf_op jit(solution)/shard_map/all_gather | solution.py:48
  62.7 49.0 %all-gather = s32[1,1,1536,8]{3,1,0,2:T(1,128)S(1)} all-gather(s32[1,1,48,8]{3,1,0,2:T(1,128)S(1)} %copy.35), channel_id=2, replica_groups=mesh['pipe'=8,'expert'=32] {'expert'}, dimensions={2}, use_global_device_ids=true | all-gather | bytes 50688 | tf_op jit(solution)/shard_map/all_gather | solution.py:48
  111.7 54.7 %fusion.42 = (s32[1536]{0:T(1024)S(1)}, s32[1536]{0:T(1024)S(1)}) fusion(s32[1,1,1536,8]{3,1,0,2:T(1,128)S(1)} %all-gather, s32[]{:T(128)S(6)} %axis_index.12, s32[1,1,1536,8]{3,1,0,2:T(1,128)S(1)} %all-gather.1), kind=kLoop, calls=%fused_computation.48 | loop fusion | flops 70656 | bytes 110596 | tf_op jit(solution)/shard_map/reduce_sum | solution.py:50
  166.9 48.6 %all-gather.2 = s32[1,1,1536,8]{3,1,0,2:T(1,128)S(1)} all-gather(s32[1,1,48,8]{3,1,0,2:T(1,128)S(1)} %copy.37), channel_id=4, replica_groups=mesh['pipe'=8,'expert'=32] {'expert'}, dimensions={2}, use_global_device_ids=true | all-gather | bytes 50688 | tf_op jit(solution)/shard_map/all_gather | solution.py:48
  215.5 27.3 %fusion.44 = s32[1536]{0:T(1024)S(1)} fusion(s32[1,1,1536,8]{3,1,0,2:T(1,128)S(1)} %all-gather.2, s32[]{:T(128)S(6)} %axis_index.12), kind=kLoop, calls=%fused_computation.50 | loop fusion | flops 35328 | bytes 55300 | tf_op jit(solution)/shard_map/reduce_sum | solution.py:50
  243.3 6.2 scatter_custom_fusion.1
  249.5 6.3 scatter_custom_fusion
  255.9 8.8 %gather_fusion = bf16[512,2048]{1,0:T(8,128)(2,1)} fusion(bf16[1536,2048]{1,0:T(8,128)(2,1)} %all-gather.7.cloned.1.call-done, s32[1024]{0:T(1024)S(1)} %pad_clamp_fusion.5), kind=kCustom, calls=%fused_computation | custom fusion | bytes 4196352 | tf_op jit(solution)/shard_map/gather | solution.py:62
  270.3 8.3 %fusion.21 = bf16[512,2048]{1,0:T(8,128)(2,1)} fusion(bf16[1,1,768,2048]{3,2,1,0:T(8,128)(2,1)S(1)} %copy-done, f32[512,768]{1,0:T(8,128)} %fusion.19, bf16[1,1,2048,768]{3,2,1,0:T(8,128)(2,1)} %param.12, bf16[512,2048]{1,0:T(8,128)(2,1)} %gather_fusion, pred[512]{0:T(512)(128)(4,1)S(1)} %broadcast_compare_fusion.5), kind=kOutput, calls=%fused_computation.39 | convolution fusion | flops 3225681920 | bytes 12059136 | tf_op jit(solution)/shard_map/dot_general | solution.py:18
  278.6 7.3 %all-to-all-start = ((bf16[32,16,2048]{2,1,0:T(8,128)(2,1)}), bf16[32,16,2048]{2,1,0:T(8,128)(2,1)}, u32[]{:S(2)}, u32[]{:S(2)}) async-start(bf16[32,16,2048]{2,1,0:T(8,128)(2,1)} %bitcast.127), calls=%async_computation | async-start | bytes 4194304 | tf_op jit(solution)/shard_map/all_to_all | solution.py:66
  288.0 27.9 %all-to-all-done = bf16[32,16,2048]{2,1,0:T(8,128)(2,1)} async-done(((bf16[32,16,2048]{2,1,0:T(8,128)(2,1)}), bf16[32,16,2048]{2,1,0:T(8,128)(2,1)}, u32[]{:S(2)}, u32[]{:S(2)}) %all-to-all-start) | async-done | bytes 2097184 | tf_op jit(solution)/shard_map/all_to_all | solution.py:66
  316.0 6.9 gather_fusion.1
  325.9 6.3 collective-permute-done
  333.3 6.2 scatter_custom_fusion.2
  339.5 6.2 scatter_custom_fusion.3
  345.7 71.4 %all-gather.9.cloned.1.call-done = bf16[1536,2048]{1,0:T(8,128)(2,1)} async-done(((bf16[48,2048]{1,0:T(8,128)(2,1)}), bf16[1536,2048]{1,0:T(8,128)(2,1)}) %all-gather.9.cloned.1.call-update) | async-done | bytes 6291472 | tf_op jit(solution)/shard_map/all_gather | solution.py:47
  417.1 9.1 %gather_fusion.2 = bf16[512,2048]{1,0:T(8,128)(2,1)} fusion(bf16[1536,2048]{1,0:T(8,128)(2,1)} %all-gather.9.cloned.1.call-done, s32[1024]{0:T(1024)S(1)} %pad_clamp_fusion.3), kind=kCustom, calls=%fused_computation.2 | custom fusion | bytes 4196352 | tf_op jit(solution)/shard_map/gather | solution.py:62
  431.7 8.3 %fusion.24 = bf16[512,2048]{1,0:T(8,128)(2,1)} fusion(bf16[1,1,768,2048]{3,2,1,0:T(8,128)(2,1)S(1)} %copy-done, f32[512,768]{1,0:T(8,128)} %fusion.17, bf16[1,1,2048,768]{3,2,1,0:T(8,128)(2,1)} %param.12, bf16[512,2048]{1,0:T(8,128)(2,1)} %gather_fusion.2, pred[512]{0:T(512)(128)(4,1)S(1)} %broadcast_compare_fusion.4), kind=kOutput, calls=%fused_computation.40 | convolution fusion | flops 3225681920 | bytes 12059136 | tf_op jit(solution)/shard_map/dot_general | solution.py:18
  440.1 5.8 all-to-all-start.1
  448.2 47.1 %all-to-all-done.1 = bf16[32,16,2048]{2,1,0:T(8,128)(2,1)} async-done(((bf16[32,16,2048]{2,1,0:T(8,128)(2,1)}), bf16[32,16,2048]{2,1,0:T(8,128)(2,1)}, u32[]{:S(2)}, u32[]{:S(2)}) %all-to-all-start.1) | async-done | bytes 2097184 | tf_op jit(solution)/shard_map/all_to_all | solution.py:66
  495.3 6.9 gather_fusion.3
  505.2 6.3 collective-permute-done.1
  512.6 6.2 scatter_custom_fusion.4
  518.8 6.2 scatter_custom_fusion.5
  525.0 72.1 %all-gather.11.cloned.1.call-done = bf16[1536,2048]{1,0:T(8,128)(2,1)} async-done(((bf16[48,2048]{1,0:T(8,128)(2,1)}), bf16[1536,2048]{1,0:T(8,128)(2,1)}) %all-gather.11.cloned.1.call-update) | async-done | bytes 6291472 | tf_op jit(solution)/shard_map/all_gather | solution.py:47
  597.2 9.0 %gather_fusion.4 = bf16[512,2048]{1,0:T(8,128)(2,1)} fusion(bf16[1536,2048]{1,0:T(8,128)(2,1)} %all-gather.11.cloned.1.call-done, s32[1024]{0:T(1024)S(1)} %pad_clamp_fusion.1), kind=kCustom, calls=%fused_computation.4 | custom fusion | bytes 4196352 | tf_op jit(solution)/shard_map/gather | solution.py:62
  606.2 5.5 fusion.15
  611.7 8.3 %fusion.27 = bf16[512,2048]{1,0:T(8,128)(2,1)} fusion(bf16[1,1,768,2048]{3,2,1,0:T(8,128)(2,1)S(1)} %copy-done, f32[512,768]{1,0:T(8,128)} %fusion.15, bf16[1,1,2048,768]{3,2,1,0:T(8,128)(2,1)} %param.12, bf16[512,2048]{1,0:T(8,128)(2,1)} %gather_fusion.4, pred[512]{0:T(512)(128)(4,1)S(1)} %broadcast_compare_fusion.3), kind=kOutput, calls=%fused_computation.41 | convolution fusion | flops 3225681920 | bytes 12059136 | tf_op jit(solution)/shard_map/dot_general | solution.py:18
  620.0 5.8 all-to-all-start.2
  627.7 47.6 %all-to-all-done.2 = bf16[32,16,2048]{2,1,0:T(8,128)(2,1)} async-done(((bf16[32,16,2048]{2,1,0:T(8,128)(2,1)}), bf16[32,16,2048]{2,1,0:T(8,128)(2,1)}, u32[]{:S(2)}, u32[]{:S(2)}) %all-to-all-start.2) | async-done | bytes 2097184 | tf_op jit(solution)/shard_map/all_to_all | solution.py:66
  675.2 6.9 gather_fusion.5
  685.1 6.3 collective-permute-done.2
  (110 shorter events, 33.9 us)
Async XLA Ops:
  6.5 263.7 %copy-start = (bf16[1,1,768,2048]{3,2,1,0:T(8,128)(2,1)S(1)}, bf16[1,1,768,2048]{3,2,1,0:T(8,128)(2,1)}, u32[]{:S(2)}) copy-start(bf16[1,1,768,2048]{3,2,1,0:T(8,128)(2,1)} %param.13) | copy-start | bytes 9437188
  6.5 249.4 %all-gather.7.cloned.1.call-start = ((), (), s32[]{:S(2)}) async-start(), calls=%async_computation.3 | async-start | bytes 6488064 | tf_op jit(solution)/shard_map/all_gather | solution.py:47
  278.6 7.6 %copy-start.3 = (f32[3,1,48,8]{2,3,1,0:T(8,128)S(1)}, f32[3,1,48,8]{2,3,1,0:T(8,128)}, u32[]{:S(2)}) copy-start(f32[3,1,48,8]{2,3,1,0:T(8,128)} %param.9) | copy-start | bytes 13828
  278.6 37.4 %all-to-all-start = ((bf16[32,16,2048]{2,1,0:T(8,128)(2,1)}), bf16[32,16,2048]{2,1,0:T(8,128)(2,1)}, u32[]{:S(2)}, u32[]{:S(2)}) async-start(bf16[32,16,2048]{2,1,0:T(8,128)(2,1)} %bitcast.127), calls=%async_computation | async-start | bytes 4194304 | tf_op jit(solution)/shard_map/all_to_all | solution.py:66
  285.9 131.2 %all-gather.9.cloned.1.call-start = ((), (), s32[]{:S(2)}) async-start(), calls=%async_computation.4 | async-start | bytes 6488064 | tf_op jit(solution)/shard_map/all_gather | solution.py:47
  322.9 2.9 copy-start.1
  322.9 9.4 %copy-start.2 = (f32[1,2048]{1,0:T(1,128)S(1)}, f32[1,2048]{1,0:T(1,128)}, u32[]{:S(2)}) copy-start(f32[1,2048]{1,0:T(1,128)} %param.10) | copy-start | bytes 24580
  325.9 6.3 collective-permute-start
  440.1 55.2 %all-to-all-start.1 = ((bf16[32,16,2048]{2,1,0:T(8,128)(2,1)}), bf16[32,16,2048]{2,1,0:T(8,128)(2,1)}, u32[]{:S(2)}, u32[]{:S(2)}) async-start(bf16[32,16,2048]{2,1,0:T(8,128)(2,1)} %bitcast.129), calls=%async_computation.1 | async-start | bytes 4194304 | tf_op jit(solution)/shard_map/all_to_all | solution.py:66
  445.9 151.3 %all-gather.11.cloned.1.call-start = ((), (), s32[]{:S(2)}) async-start(), calls=%async_computation.5 | async-start | bytes 6488064 | tf_op jit(solution)/shard_map/all_gather | solution.py:47
  505.2 6.3 collective-permute-start.1
  620.0 55.2 %all-to-all-start.2 = ((bf16[32,16,2048]{2,1,0:T(8,128)(2,1)}), bf16[32,16,2048]{2,1,0:T(8,128)(2,1)}, u32[]{:S(2)}, u32[]{:S(2)}) async-start(bf16[32,16,2048]{2,1,0:T(8,128)(2,1)} %bitcast.128), calls=%async_computation.2 | async-start | bytes 4194304 | tf_op jit(solution)/shard_map/all_to_all | solution.py:66
  685.1 6.3 collective-permute-start.2
Sparse Core Ops, SparseCore 0:
  9.9 92.9 all-gather.6
  333.3 83.7 all-gather.8
  512.6 84.5 all-gather.10
where the time goes:
time: 711 us; the launch traced here: 699 us
  waiting for transfers between devices  285 us (40%)
  blocking collectives  150 us (21%)
  other arithmetic  101 us (14%)
  local copies, waits for them, and re-layouts  89 us (13%)
  matrix products  41.6 us (6%)
  starting transfers between devices  19.1 us (3%)
  between operations  13.8 us (2%)
    all_gather x3, blocking collectives, shards(): lax.all_gather(section_ids, 'expert', axis=0, tiled=True)  150 us
    all_gather x3, waiting for transfers between devices, shards(): lax.all_gather(normed, 'expert', axis=0, tiled=True)  144 us
    all_to_all x3, waiting for transfers between devices, shards(): lax.all_to_all(results, 'expert', split_axis=0, concat_axis=0, tiled=True)  123 us
    reduce_sum x2, other arithmetic, shards(): hit_token = jnp.sum((all_ids == owner).astype(jnp.int32), axis=1)  82 us
    gather x3, local copies, waits for them, and re-layouts, shards(): all_rows[slot_token]  26.9 us
    dot_general x3, matrix products, expert_ffn(): jnp.dot(hidden, down_weight, preferred_element_type=jnp.float32)  25 us
    gather x3, local copies, waits for them, and re-layouts, shards(): returned.reshape(experts * capacity, width)[position]  20.8 us
    all_to_all x3, starting transfers between devices, shards(): lax.all_to_all(results, 'expert', split_axis=0, concat_axis=0, tiled=True)  19 us
  transfers between devices with their start and end apart: 9, of which 8 were waited for; matrix products, arithmetic and copies ran while one was open for 18% of the time, Pallas kernels for 0%

commit v1 on v0

v1 whole, which is shorter than its diff:
```python
import functools

import jax
import jax.numpy as jnp
from jax import lax
from jax.experimental import pallas as pl
from jax.experimental.pallas import tpu as pltpu
from jax.sharding import PartitionSpec as P

F32 = jnp.float32
BF16 = jnp.bfloat16


def iota(shape, axis):
    return lax.broadcasted_iota(jnp.int32, shape, axis)


def table_kernel(experts, ids_ref, idst_ref, wts_ref, sel_ref, comb_ref):
    rows, chosen = ids_ref.shape[1], ids_ref.shape[2]
    places = sel_ref.shape[1]
    cap = places // experts
    hit_t = jnp.zeros((experts, rows), F32)
    hit = jnp.zeros((rows, experts), F32)
    weight = jnp.zeros((rows, experts), F32)
    for k in range(chosen):
        hit_t += (idst_ref[0, k : k + 1, :] == iota((experts, rows), 0)).astype(F32)
        here = ids_ref[0, :, k : k + 1] == iota((rows, experts), 1)
        hit += here.astype(F32)
        weight += jnp.where(here, wts_ref[0, :, k : k + 1], 0.0)
    before_t = (iota((rows, rows), 0) < iota((rows, rows), 1)).astype(BF16)
    before = (iota((rows, rows), 1) < iota((rows, rows), 0)).astype(BF16)
    rank_t = jnp.dot(hit_t.astype(BF16), before_t, preferred_element_type=F32)
    rank = jnp.dot(before, hit.astype(BF16), preferred_element_type=F32)
    code_t = jnp.where(hit_t > 0, rank_t, -1.0).astype(BF16)
    code = jnp.where(hit > 0, rank, -1.0).astype(BF16)
    high = weight.astype(BF16)
    low = (weight - high.astype(F32)).astype(BF16)
    spread_t = (iota((places, experts), 0) // cap == iota((places, experts), 1)).astype(BF16)
    spread = (iota((experts, places), 1) // cap == iota((experts, places), 0)).astype(BF16)
    slot_t = jnp.dot(spread_t, code_t, preferred_element_type=F32)
    slot = jnp.dot(code, spread, preferred_element_type=F32)
    want_t = (iota((places, rows), 0) % cap).astype(F32)
    want = (iota((rows, places), 1) % cap).astype(F32)
    sel_ref[0] = (slot_t == want_t).astype(BF16)
    for part, value in ((0, high), (1, low)):
        wide = jnp.dot(value, spread, preferred_element_type=F32)
        comb_ref[0, part * rows : (part + 1) * rows, :] = jnp.where(slot == want, wide, 0.0).astype(BF16)


def tables(ids, wts, experts, cap):
    ticks, rows, chosen = ids.shape
    places = experts * cap
    return pl.pallas_call(
        functools.partial(table_kernel, experts),
        grid=(ticks,),
        in_specs=[
            pl.BlockSpec((1, rows, chosen), lambda t: (t, 0, 0)),
            pl.BlockSpec((1, chosen, rows), lambda t: (t, 0, 0)),
            pl.BlockSpec((1, rows, chosen), lambda t: (t, 0, 0)),
        ],
        out_specs=[
            pl.BlockSpec((1, places, rows), lambda t: (t, 0, 0)),
            pl.BlockSpec((1, 2 * rows, places), lambda t: (t, 0, 0)),
        ],
        out_shape=[
            jax.ShapeDtypeStruct((ticks, places, rows), BF16),
            jax.ShapeDtypeStruct((ticks, 2 * rows, places), BF16),
        ],
        name="tables",
    )(ids, ids.transpose(0, 2, 1), wts)


def slot_kernel(x_ref, gain_ref, sel_ref, out_ref):
    wide = x_ref[...].astype(F32)
    scale = lax.rsqrt(jnp.mean(wide * wide, axis=-1, keepdims=True) + 1e-06)
    normed = (wide * scale * gain_ref[...]).astype(BF16)
    out_ref[...] = jnp.dot(sel_ref[...], normed, preferred_element_type=F32).astype(BF16)


def slotted(x, gain, sel):
    return pl.pallas_call(
        slot_kernel,
        out_shape=jax.ShapeDtypeStruct((sel.shape[0], x.shape[1]), BF16),
        name="slotted",
    )(x, gain, sel)


def ffn_kernel(x_ref, gate_ref, up_ref, down_ref, out_ref, acc_ref):
    step = pl.program_id(0)
    x = x_ref[...]
    gate = jnp.dot(x, gate_ref[...], preferred_element_type=F32)
    upper = jnp.dot(x, up_ref[...], preferred_element_type=F32)
    hidden = (gate / (1.0 + jnp.exp(-gate)) * upper).astype(BF16)
    part = jnp.dot(hidden, down_ref[...], preferred_element_type=F32)
    last = pl.num_programs(0) - 1

    @pl.when(step == 0)
    def _():
        acc_ref[...] = part

    @pl.when((step > 0) & (step < last))
    def _():
        acc_ref[...] += part

    @pl.when(step == last)
    def _():
        out_ref[...] = (acc_ref[...] + part).astype(BF16)


def ffn(x, gate, up, down):
    rows, width = x.shape
    hidden = gate.shape[1]
    block = 256
    return pl.pallas_call(
        ffn_kernel,
        grid=(hidden // block,),
        in_specs=[
            pl.BlockSpec((rows, width), lambda f: (0, 0)),
            pl.BlockSpec((width, block), lambda f: (0, f)),
            pl.BlockSpec((width, block), lambda f: (0, f)),
            pl.BlockSpec((block, width), lambda f: (f, 0)),
        ],
        out_specs=pl.BlockSpec((rows, width), lambda f: (0, 0)),
        out_shape=jax.ShapeDtypeStruct((rows, width), BF16),
        scratch_shapes=[pltpu.VMEM((rows, width), F32)],
        compiler_params=pltpu.CompilerParams(vmem_limit_bytes=48 << 20),
        cost_estimate=pl.CostEstimate(
            flops=6 * rows * width * hidden,
            bytes_accessed=6 * width * hidden + 4 * rows * width,
            transcendentals=rows * hidden,
        ),
        name="ffn",
    )(x, gate, up, down)


def combine_kernel(x_ref, back_ref, comb_ref, out_ref):
    rows = x_ref.shape[0]
    both = jnp.dot(comb_ref[...], back_ref[...], preferred_element_type=F32)
    out_ref[...] = (x_ref[...].astype(F32) + (both[:rows] + both[rows:])).astype(BF16)


def combined(x, back, comb):
    return pl.pallas_call(
        combine_kernel,
        out_shape=jax.ShapeDtypeStruct(x.shape, BF16),
        name="combined",
    )(x, back, comb)


def shards(state, route_ids, route_weights, norm_gain, w_gate, w_up, w_down):
    experts = lax.axis_size("expert")
    sections = lax.axis_size("pipe")
    panel = state[0]
    rows, width = panel.shape
    cap = 16
    sel, comb = tables(route_ids[:, 0], route_weights[:, 0], experts, cap)
    ring = [(i, (i + 1) % sections) for i in range(sections)]
    for tick in range(route_ids.shape[0]):
        outgoing = slotted(panel, norm_gain, sel[tick])
        incoming = lax.all_to_all(
            outgoing.reshape(experts, cap, width), "expert", split_axis=0, concat_axis=0, tiled=True
        )
        results = ffn(incoming.reshape(experts * cap, width), w_gate[0, 0], w_up[0, 0], w_down[0, 0])
        back = lax.all_to_all(
            results.reshape(experts, cap, width), "expert", split_axis=0, concat_axis=0, tiled=True
        )
        updated = combined(panel, back.reshape(experts * cap, width), comb[tick])
        panel = lax.ppermute(updated, "pipe", ring)
    return panel[None]


def solution(mesh):
    placed = (
        P("pipe", "expert", None),
        P(None, "pipe", "expert", None),
        P(None, "pipe", "expert", None),
        P("pipe", None),
        P("pipe", "expert", None, None),
        P("pipe", "expert", None, None),
        P("pipe", "expert", None, None),
    )
    return jax.shard_map(
        shards, mesh=mesh, in_specs=placed, out_specs=P("pipe", "expert", None), check_vma=False
    )
```

time: 711 us -> 414 us (0.58); the launches traced: 699 us -> 413 us
  waiting for transfers between devices: 285 us -> 67.9 us
  blocking collectives: 150 us -> 284 us
  other arithmetic: 101 us -> 0 us
  local copies, waits for them, and re-layouts: 89 us -> 8.72 us
  Pallas kernels: 0 us -> 47.2 us
  matrix products: 41.6 us -> 0 us
  starting transfers between devices: 19.1 us -> 5.34 us
  between operations: 13.8 us -> 0.05 us
    all_to_all x0 -> x5, blocking collectives: none -> 284 us  [the longest x3 174 us: shards(): lax.all_to_all(outgoing.reshape(experts, cap, width), 'expert', split_axi...]
    all_gather x3 -> x0, blocking collectives: 150 us -> none  [shards(): lax.all_gather(section_ids, 'expert', axis=0, tiled=True)]
    all_gather x3 -> x0, waiting for transfers between devices: 144 us -> none  [shards(): lax.all_gather(normed, 'expert', axis=0, tiled=True)]
    reduce_sum x11 -> x0, other arithmetic: 92.4 us -> none  [the longest x2 82 us: shards(): hit_token = jnp.sum((all_ids == owner).astype(jnp.int32), axis=1)]
    all_to_all x3 -> x1, waiting for transfers between devices: 123 us -> 48.4 us  [shards(): lax.all_to_all(results.reshape(experts, cap, width), 'expert', split_axis...]
    gather x6 -> x0, local copies, waits for them, and re-layouts: 47.7 us -> none  [the longest x3 26.9 us: shards(): all_rows[slot_token]]
    pallas_call x0 -> x10, Pallas kernels: none -> 47.2 us  [the longest x3 26.4 us: ffn(): pl.pallas_call(ffn_kernel, grid=(hidden // block,), in_specs=[pl.BlockSpe...]
    dot_general x6 -> x0, matrix products: 41.6 us -> none  [the longest x3 25 us: expert_ffn(): jnp.dot(hidden, down_weight, preferred_element_type=jnp.float32)]
  transfers between devices with their start and end apart: 9 -> 4, of which waited for: 8 -> 4; matrix products, arithmetic and copies ran while one was open for 18% -> 0% of each run, Pallas kernels for 0% -> 0%
where the time goes in v1:
time: 414 us; the launch traced here: 413 us
  blocking collectives  284 us (69%)
  waiting for transfers between devices  67.9 us (16%)
  Pallas kernels  47.2 us (11%)
  local copies, waits for them, and re-layouts  8.72 us (2%)
  starting transfers between devices  5.34 us (1%)
    all_to_all x3, blocking collectives, shards(): lax.all_to_all(outgoing.reshape(experts, cap, width), 'expert', split_axi...  174 us
    all_to_all x2, blocking collectives, shards(): lax.all_to_all(results.reshape(experts, cap, width), 'expert', split_axis...  109 us
    all_to_all x1, waiting for transfers between devices, shards(): lax.all_to_all(results.reshape(experts, cap, width), 'expert', split_axis...  48.4 us
    pallas_call x3, Pallas kernels, ffn(): pl.pallas_call(ffn_kernel, grid=(hidden // block,), in_specs=[pl.BlockSpe...  26.4 us
    ppermute x3, waiting for transfers between devices, shards(): panel = lax.ppermute(updated, 'pipe', ring)  19.5 us
    pallas_call x3, Pallas kernels, slotted(): pl.pallas_call(slot_kernel, out_shape=jax.ShapeDtypeStruct((sel.shape[0],...  9.45 us
  transfers between devices with their start and end apart: 4, of which 4 were waited for; matrix products, arithmetic and copies ran while one was open for 0% of the time, Pallas kernels for 0%

profile of v1, /device:TPU:32, one launch (start us, length us, event | category | flops | bytes accessed | tf_op | source)
XLA Modules:
  0.0 412.8 jit_solution(12313453143511425473)
XLA Ops:
  0.0 1.4 copy.8
  1.4 1.4 copy.9.ids_ref
  2.8 3.1 tables.1
  6.0 1.8 slice_bitcast_fusion
  7.8 3.1 slotted.3
  10.9 62.2 %all_to_all.30 = bf16[32,16,2048]{2,1,0:T(8,128)(2,1)S(1)} all-to-all(bf16[32,16,2048]{2,1,0:T(8,128)(2,1)} %bitcast.41), channel_id=1, replica_groups=mesh['pipe'=8,'expert'=32] {'expert'}, dimensions={0} | all-to-all | bytes 4194304 | tf_op jit(solution)/shard_map/all_to_all | solution.py:160
  73.1 9.7 %ffn.3 = bf16[512,2048]{1,0:T(8,128)(2,1)} custom-call(bf16[512,2048]{1,0:T(8,128)(2,1)S(1)} %bitcast.33, bf16[2048,768]{1,0:T(8,128)(2,1)} %bitcast.50, bf16[2048,768]{1,0:T(8,128)(2,1)} %bitcast.53, bf16[768,2048]{1,0:T(8,128)(2,1)} %bitcast.56), custom_call_target="tpu_custom_call" | custom-call | flops 4831838208 | bytes 13631488 | tf_op jit(solution)/shard_map/ffn/pallas_call | solution.py:114
  82.8 5.3 %all-to-all-start.1 = ((bf16[32,16,2048]{2,1,0:T(8,128)(2,1)}), bf16[32,16,2048]{2,1,0:T(8,128)(2,1)S(1)}, u32[]{:S(2)}, u32[]{:S(2)}) async-start(bf16[32,16,2048]{2,1,0:T(8,128)(2,1)} %bitcast.10), calls=%async_computation.1 | async-start | bytes 4194304 | tf_op jit(solution)/shard_map/all_to_all | solution.py:164
  88.1 0.0 copy-done.3
  88.1 0.7 slice_bitcast_fusion.3
  88.9 48.4 %all-to-all-done.1 = bf16[32,16,2048]{2,1,0:T(8,128)(2,1)S(1)} async-done(((bf16[32,16,2048]{2,1,0:T(8,128)(2,1)}), bf16[32,16,2048]{2,1,0:T(8,128)(2,1)S(1)}, u32[]{:S(2)}, u32[]{:S(2)}) %all-to-all-start.1) | async-done | bytes 2097184 | tf_op jit(solution)/shard_map/all_to_all | solution.py:164
  137.2 1.3 copy-done
  138.6 2.7 combined.3
  141.3 0.0 collective-permute-start
  141.3 6.5 %collective-permute-done.x_ref = bf16[48,2048]{1,0:T(8,128)(2,1)S(1)} collective-permute-done((bf16[48,2048]{1,0:T(8,128)(2,1)}, bf16[48,2048]{1,0:T(8,128)(2,1)S(1)}, u32[]{:S(2)}, u32[]{:S(2)}) %collective-permute-start) | collective-permute-done | bytes 196640 | tf_op jit(solution)/shard_map/ppermute | solution.py:168
  147.8 0.7 copy-done.2
  148.5 3.2 slotted.4
  151.7 55.9 %all_to_all.31 = bf16[32,16,2048]{2,1,0:T(8,128)(2,1)S(1)} all-to-all(bf16[32,16,2048]{2,1,0:T(8,128)(2,1)} %bitcast.42), channel_id=1, replica_groups=mesh['pipe'=8,'expert'=32] {'expert'}, dimensions={0} | all-to-all | bytes 4194304 | tf_op jit(solution)/shard_map/all_to_all | solution.py:160
  207.5 8.4 %ffn.4 = bf16[512,2048]{1,0:T(8,128)(2,1)S(1)} custom-call(bf16[512,2048]{1,0:T(8,128)(2,1)S(1)} %bitcast.34, bf16[2048,768]{1,0:T(8,128)(2,1)} %bitcast.51, bf16[2048,768]{1,0:T(8,128)(2,1)} %bitcast.54, bf16[768,2048]{1,0:T(8,128)(2,1)} %bitcast.57), custom_call_target="tpu_custom_call" | custom-call | flops 4831838208 | bytes 13631488 | tf_op jit(solution)/shard_map/ffn/pallas_call | solution.py:114
  215.9 53.5 %all_to_all.32 = bf16[32,16,2048]{2,1,0:T(8,128)(2,1)} all-to-all(bf16[32,16,2048]{2,1,0:T(8,128)(2,1)S(1)} %bitcast.35), channel_id=1, replica_groups=mesh['pipe'=8,'expert'=32] {'expert'}, dimensions={0} | all-to-all | bytes 4194304 | tf_op jit(solution)/shard_map/all_to_all | solution.py:164
  269.4 2.7 combined.4
  272.1 0.0 collective-permute-start.1
  272.1 6.5 %collective-permute-done.1.x_ref = bf16[48,2048]{1,0:T(8,128)(2,1)S(1)} collective-permute-done((bf16[48,2048]{1,0:T(8,128)(2,1)}, bf16[48,2048]{1,0:T(8,128)(2,1)S(1)}, u32[]{:S(2)}, u32[]{:S(2)}) %collective-permute-start.1) | collective-permute-done | bytes 196640 | tf_op jit(solution)/shard_map/ppermute | solution.py:168
  278.7 0.7 copy-done.1
  279.3 3.2 slotted.5
  282.5 56.4 %all_to_all.33 = bf16[32,16,2048]{2,1,0:T(8,128)(2,1)S(1)} all-to-all(bf16[32,16,2048]{2,1,0:T(8,128)(2,1)} %bitcast.43), channel_id=1, replica_groups=mesh['pipe'=8,'expert'=32] {'expert'}, dimensions={0} | all-to-all | bytes 4194304 | tf_op jit(solution)/shard_map/all_to_all | solution.py:160
  338.9 8.4 %ffn.5 = bf16[512,2048]{1,0:T(8,128)(2,1)S(1)} custom-call(bf16[512,2048]{1,0:T(8,128)(2,1)S(1)} %bitcast.36, bf16[2048,768]{1,0:T(8,128)(2,1)} %bitcast.52, bf16[2048,768]{1,0:T(8,128)(2,1)} %bitcast.55, bf16[768,2048]{1,0:T(8,128)(2,1)} %bitcast.58), custom_call_target="tpu_custom_call" | custom-call | flops 4831838208 | bytes 13631488 | tf_op jit(solution)/shard_map/ffn/pallas_call | solution.py:114
  347.3 55.6 %all_to_all.34 = bf16[32,16,2048]{2,1,0:T(8,128)(2,1)} all-to-all(bf16[32,16,2048]{2,1,0:T(8,128)(2,1)S(1)} %bitcast.37), channel_id=1, replica_groups=mesh['pipe'=8,'expert'=32] {'expert'}, dimensions={0} | all-to-all | bytes 4194304 | tf_op jit(solution)/shard_map/all_to_all | solution.py:164
  402.9 2.7 combined.5
  405.6 0.0 collective-permute-start.2
  405.6 6.5 %collective-permute-done.2 = bf16[48,2048]{1,0:T(8,128)(2,1)S(1)} collective-permute-done((bf16[48,2048]{1,0:T(8,128)(2,1)}, bf16[48,2048]{1,0:T(8,128)(2,1)S(1)}, u32[]{:S(2)}, u32[]{:S(2)}) %collective-permute-start.2) | collective-permute-done | bytes 196640 | tf_op jit(solution)/shard_map/ppermute | solution.py:168
  412.1 0.7 copy.11
  (4 shorter events, 0.0 us)
Async XLA Ops:
  82.8 5.3 %copy-start.3 = (bf16[3,96,512]{2,1,0:T(8,128)(2,1)S(1)}, bf16[3,96,512]{2,1,0:T(8,128)(2,1)}, u32[]{:S(2)}) copy-start(bf16[3,96,512]{2,1,0:T(8,128)(2,1)} %get-tuple-element.8) | copy-start | bytes 884740
  82.8 54.5 %all-to-all-start.1 = ((bf16[32,16,2048]{2,1,0:T(8,128)(2,1)}), bf16[32,16,2048]{2,1,0:T(8,128)(2,1)S(1)}, u32[]{:S(2)}, u32[]{:S(2)}) async-start(bf16[32,16,2048]{2,1,0:T(8,128)(2,1)} %bitcast.10), calls=%async_computation.1 | async-start | bytes 4194304 | tf_op jit(solution)/shard_map/all_to_all | solution.py:164
  137.2 1.3 copy-start
  141.3 6.5 %collective-permute-start = (bf16[48,2048]{1,0:T(8,128)(2,1)}, bf16[48,2048]{1,0:T(8,128)(2,1)S(1)}, u32[]{:S(2)}, u32[]{:S(2)}) collective-permute-start(bf16[48,2048]{1,0:T(8,128)(2,1)} %combined.3), channel_id=1, source_target_pairs={{0,32},{32,64},{64,96},{96,128},{128,160},{160,192},{192,224},{224... | collective-permute-start | bytes 589832 | tf_op jit(solution)/shard_map/ppermute | solution.py:168
  147.8 0.7 copy-start.2
  272.1 6.5 %collective-permute-start.1 = (bf16[48,2048]{1,0:T(8,128)(2,1)}, bf16[48,2048]{1,0:T(8,128)(2,1)S(1)}, u32[]{:S(2)}, u32[]{:S(2)}) collective-permute-start(bf16[48,2048]{1,0:T(8,128)(2,1)} %combined.4), channel_id=1, source_target_pairs={{0,32},{32,64},{64,96},{96,128},{128,160},{160,192},{192,224},{224... | collective-permute-start | bytes 589832 | tf_op jit(solution)/shard_map/ppermute | solution.py:168
  278.7 0.7 copy-start.1
  405.6 6.5 %collective-permute-start.2 = (bf16[48,2048]{1,0:T(8,128)(2,1)}, bf16[48,2048]{1,0:T(8,128)(2,1)S(1)}, u32[]{:S(2)}, u32[]{:S(2)}) collective-permute-start(bf16[48,2048]{1,0:T(8,128)(2,1)} %combined.5), channel_id=1, source_target_pairs={{0,32},{32,64},{64,96},{96,128},{128,160},{160,192},{192,224},{224... | collective-permute-start | bytes 589832 | tf_op jit(solution)/shard_map/ppermute | solution.py:168
